TPU v7x, 512 devices: a whole 4x4x16 slice. The times are simulated.
512 devices in a mesh: lat: 64 (over y, z), wid: 8 (over x, core).
Axes of the slice: x: 4, y: 4, z: 16, core: 2. Of those that a mesh axis runs over, the one named last changes fastest.
Arguments:
- activations: bfloat16 [128, 3584], P(None, 'wid'), may hold values from -6 to 6
- encoder: bfloat16 [3584, 32768], P('wid', 'lat'), may hold values from -0.09375 to 0.09375
- encoder_bias: float32 [32768], P('lat'), may hold values from -3 to 3
- decoder: bfloat16 [32768, 3584], P('lat', 'wid'), may hold values from -0.75 to 0.75
- decoder_bias: float32 [3584], P('wid'), may hold values from -3 to 3
- kept_mask: int32 [128, 32768], P(None, 'lat'), may hold values 0 or 1
- boundaries: int32 [8], replicated, may hold values from 4097 to 32768, as said below
Outputs:
- encoder_grad: bfloat16 [3584, 32768], P('wid', 'lat')
- encoder_bias_grad: float32 [32768], P('lat')
- decoder_grad: bfloat16 [32768, 3584], P('lat', 'wid')
- decoder_bias_grad: float32 [3584], P('wid')
Inputs may be any that keep to these rules, and one draw needn't show every extreme that they name: `boundaries`: Rising; for k below 7, boundary k lies among the 512 latents that follow (k + 1) * 4096; the last equals 32768.
All inputs are finite; a program needn't handle non-finite values. No bound on the sum of `kept_mask` on one device may be relied on, other than what follows from the above.
Results may differ from a plain program's by a relative error of at most 0.006.
Values may be sent and summed in bfloat16 or wider, within the bound.
No kernel may reach another device: no remote copies, remote signals or barrier semaphores. Data moves between devices by JAX's collectives and lax.ppermute only.
A program may use at most 128 MiB of HBM per device.

v0:
```python
import jax
import jax.numpy as jnp
from jax import lax
from jax.sharding import PartitionSpec as P

GROUPS = 8


def prefix(part, axis, combine, identity, reverse):
    count = lax.axis_size(axis)
    place = lax.axis_index(axis)
    ahead = count - 1 - place if reverse else place
    gathered = lax.all_gather(part, axis)
    state = jnp.zeros_like(part) + jnp.asarray(identity, part.dtype)

    def one(step, state):
        source = count - 1 - step if reverse else step
        return combine(state, lax.dynamic_index_in_dim(gathered, source, 0, False))

    return lax.fori_loop(0, ahead, one, state)


def add_terms(earlier, later):
    return earlier + later


def body(activations, encoder, encoder_bias, decoder, decoder_bias, kept_mask, boundaries):
    latent_width = encoder.shape[1]
    first_latent = lax.axis_index("lat") * latent_width
    latent_ids = first_latent + jnp.arange(latent_width, dtype=jnp.int32)
    kept_float = kept_mask.astype(jnp.float32)
    encoder_part = jnp.dot(activations, encoder, preferred_element_type=jnp.float32)
    preacts = lax.psum(encoder_part, "wid") + encoder_bias
    codes = (kept_float * preacts).astype(jnp.bfloat16)
    inside_rows = (boundaries > first_latent) & (boundaries <= first_latent + latent_width)
    holds_cut = jnp.any(inside_rows)
    cut_point = jnp.sum(jnp.where(inside_rows, boundaries, 0))
    below_cut = latent_ids < cut_point
    zero_code = jnp.zeros((), jnp.bfloat16)
    masked_codes = jnp.stack(
        [
            jnp.where(below_cut[None, :], codes, zero_code),
            jnp.where(below_cut[None, :], zero_code, codes),
        ]
    )
    decoded_pieces = jnp.einsum(
        "sbj,jd->sbd", masked_codes, decoder, preferred_element_type=jnp.float32
    )
    local_total = decoded_pieces[0] + decoded_pieces[1]
    zero_rows = jnp.zeros_like(local_total)
    prefix_sum = prefix(local_total, "lat", add_terms, zero_rows, False)
    target_rows = activations.astype(jnp.float32)
    scaled_error = jnp.where(
        holds_cut, (decoder_bias + prefix_sum + decoded_pieces[0] - target_rows) / GROUPS, 0.0
    )
    suffix_sum = prefix(scaled_error, "lat", add_terms, zero_rows, True)
    below_suffix = suffix_sum + scaled_error
    suffix_pair = jnp.stack([below_suffix, suffix_sum]).astype(jnp.bfloat16)
    back_grads = jnp.einsum("sbd,jd->sbj", suffix_pair, decoder, preferred_element_type=jnp.float32)
    partial_grads = jnp.where(below_cut[None, :], back_grads[0], back_grads[1])
    coded_grads = lax.psum(partial_grads, "wid")
    pre_grads = kept_float * coded_grads
    encoder_bias_grad = jnp.sum(pre_grads, axis=0)
    pre_low = pre_grads.astype(jnp.bfloat16)
    encoder_grad = lax.dot_general(
        activations, pre_low, (((0,), (0,)), ((), ())), preferred_element_type=jnp.float32
    ).astype(jnp.bfloat16)
    decoder_grad = jnp.einsum(
        "sbj,sbd->jd", masked_codes, suffix_pair, preferred_element_type=jnp.float32
    ).astype(jnp.bfloat16)
    decoder_bias_grad = lax.psum(jnp.sum(scaled_error, axis=0), "lat")
    return (encoder_grad, encoder_bias_grad, decoder_grad, decoder_bias_grad)


def solution(mesh):
    placed = (
        P(None, "wid"),
        P("wid", "lat"),
        P("lat"),
        P("lat", "wid"),
        P("wid"),
        P(None, "lat"),
        P(),
    )
    return jax.shard_map(
        body,
        mesh=mesh,
        in_specs=placed,
        out_specs=(P("wid", "lat"), P("lat"), P("lat", "wid"), P("wid")),
        check_vma=False,
    )
```

profile of v0, /device:TPU:32, one launch (start us, length us, event | category | flops | bytes accessed | tf_op | source)
XLA Modules:
  0.0 781.7 jit_solution(4494470858266741804)
XLA Ops:
  7.2 2.1 fusion.19
  9.4 1.3 select_reduce_fusion
  11.3 78.9 %all-reduce.3.cloned.1.call-done = f32[128,512]{1,0:T(8,128)} async-done(((f32[128,512]{1,0:T(8,128)}), f32[128,512]{1,0:T(8,128)}) %all-reduce.3.cloned.1.call-update) | async-done | bytes 262160 | tf_op jit(solution)/shard_map/psum | solution.py:33
  90.2 1.1 select_bitcast_fusion.1
  92.5 1.3 fusion.16
  93.8 180.1 %all-gather.4.cloned.1.call-done = f32[64,128,448]{1,2,0:T(8,128)} async-done(((f32[1,128,448]{1,2,0:T(8,128)}), f32[64,128,448]{1,2,0:T(8,128)}) %all-gather.4.cloned.1.call-update) | async-done | bytes 14680080 | tf_op jit(solution)/shard_map/all_gather | solution.py:13
  273.8 1.2 while.22
  275.2 2.4 fusion.17
  277.7 269.5 %all-gather.6.cloned.1.call-done = f32[8192,448]{0,1:T(8,128)} async-done(((f32[128,448]{0,1:T(8,128)}), f32[8192,448]{0,1:T(8,128)}) %all-gather.6.cloned.1.call-update) | async-done | bytes 14680080 | tf_op jit(solution)/shard_map/all_gather | solution.py:13
  547.1 16.6 %copy.25 = f32[8192,448]{1,0:T(8,128)} copy(f32[8192,448]{0,1:T(8,128)} %all-gather.6.cloned.1.call-done) | data formatting | bytes 29360128 | tf_op jit(solution)/shard_map/while | solution.py:20
  563.7 65.1 %while.23 = (s32[]{:T(128)}, f32[128,448]{1,0:T(8,128)S(1)}, s32[]{:T(128)}, f32[64,128,448]{2,1,0:T(8,128)}, s32[]{:T(128)}, /*index=5*/s32[]{:T(128)}, s32[]{:T(128)}, s32[]{:T(128)}) while((s32[]{:T(128)}, f32[128,448]{1,0:T(8,128)S(1)}, s32[]{:T(128)}, f32[64,128,448]{2,1,0:T(8,128)}, s32[]{:T(128)}, /*index=5*/s32[]{:T(128)}, s32[]{:T(128)}, ...), condition=%wide.region_6.7_spmd, body=%wide.region_5.6_spmd.sunk | while | flops 57350 | bytes 688263 | solution.py:20
  563.8 1.0 bitcast_add_fusion.6
  564.8 1.0 bitcast_add_fusion.6
  565.9 1.0 bitcast_add_fusion.6
  566.9 1.0 bitcast_add_fusion.6
  568.0 1.0 bitcast_add_fusion.6
  569.0 1.0 bitcast_add_fusion.6
  570.0 1.0 bitcast_add_fusion.6
  571.1 1.0 bitcast_add_fusion.6
  572.1 1.0 bitcast_add_fusion.6
  573.2 1.0 bitcast_add_fusion.6
  574.2 1.0 bitcast_add_fusion.6
  575.3 1.0 bitcast_add_fusion.6
  576.3 1.0 bitcast_add_fusion.6
  577.4 1.0 bitcast_add_fusion.6
  578.4 1.0 bitcast_add_fusion.6
  579.5 1.0 bitcast_add_fusion.6
  580.5 1.0 bitcast_add_fusion.6
  581.6 1.0 bitcast_add_fusion.6
  582.6 1.0 bitcast_add_fusion.6
  583.7 1.0 bitcast_add_fusion.6
  584.7 1.0 bitcast_add_fusion.6
  585.8 1.0 bitcast_add_fusion.6
  586.8 1.0 bitcast_add_fusion.6
  587.9 1.0 bitcast_add_fusion.6
  588.9 1.0 bitcast_add_fusion.6
  590.0 1.0 bitcast_add_fusion.6
  591.0 1.0 bitcast_add_fusion.6
  592.1 1.0 bitcast_add_fusion.6
  593.1 1.0 bitcast_add_fusion.6
  594.2 1.0 bitcast_add_fusion.6
  595.2 1.0 bitcast_add_fusion.6
  596.3 1.0 bitcast_add_fusion.6
  597.3 1.0 bitcast_add_fusion.6
  598.4 1.0 bitcast_add_fusion.6
  599.4 1.0 bitcast_add_fusion.6
  600.5 1.0 bitcast_add_fusion.6
  601.5 1.0 bitcast_add_fusion.6
  602.6 1.0 bitcast_add_fusion.6
  603.6 1.0 bitcast_add_fusion.6
  604.7 1.0 bitcast_add_fusion.6
  605.7 1.0 bitcast_add_fusion.6
  606.8 1.0 bitcast_add_fusion.6
  607.8 1.0 bitcast_add_fusion.6
  608.9 1.0 bitcast_add_fusion.6
  613.1 1.0 bitcast_add_fusion.6
  616.2 1.0 bitcast_add_fusion.6
  619.4 1.0 bitcast_add_fusion.6
  622.5 1.0 bitcast_add_fusion.6
  625.7 1.0 bitcast_add_fusion.6
  630.1 140.5 %psum.23 = f32[448]{0:T(512)} all-reduce(f32[448]{0:T(512)S(1)} %get-tuple-element.117), channel_id=1, replica_groups=mesh['lat'=64,'wid'=8] {'lat'}, use_global_device_ids=true, to_apply=%region_10.11 | all-reduce | flops 448 | bytes 3584 | tf_op jit(solution)/shard_map/psum | solution.py:71
  770.5 1.1 fusion
  771.6 2.0 fusion.1
  773.6 1.6 fusion.11
  (44 shorter events, 17.8 us)
Async XLA Ops:
  7.2 84.2 %copy-start = (bf16[512,448]{0,1:T(8,128)(2,1)S(1)}, bf16[512,448]{0,1:T(8,128)(2,1)}, u32[]{:S(2)}) copy-start(bf16[512,448]{0,1:T(8,128)(2,1)} %param.14) | copy-start | bytes 1376260
  7.2 83.0 %all-reduce.3.cloned.1.call-start = ((), (), s32[]{:S(2)}) async-start(), calls=%async_computation | async-start | bytes 524288 | tf_op jit(solution)/shard_map/psum | solution.py:33
  9.3 264.5 %all-gather.4.cloned.1.call-start = ((), (), s32[]{:S(2)}) async-start(), calls=%async_computation.1 | async-start | bytes 14909440 | tf_op jit(solution)/shard_map/all_gather | solution.py:13
  92.4 454.7 %all-gather.6.cloned.1.call-start = ((), (), s32[]{:S(2)}) async-start(), calls=%async_computation.3 | async-start | bytes 14909440 | tf_op jit(solution)/shard_map/all_gather | solution.py:13
  277.6 494.0 %all-reduce.5.cloned.1.call-start = ((), (), s32[]{:S(2)}) async-start(), calls=%async_computation.2 | async-start | bytes 524288 | tf_op jit(solution)/shard_map/psum | solution.py:61
  277.6 351.3 %copy-start.2 = (f32[128,448]{0,1:T(8,128)S(1)}, f32[128,448]{0,1:T(8,128)}, u32[]{:S(2)}) copy-start(f32[128,448]{0,1:T(8,128)} %get-tuple-element.118) | copy-start | bytes 688132
  277.6 494.0 %copy-start.1 = (s32[128,512]{1,0:T(8,128)S(1)}, s32[128,512]{1,0:T(8,128)}, u32[]{:S(2)}) copy-start(s32[128,512]{1,0:T(8,128)} %param.16) | copy-start | bytes 786436
  277.6 493.9 %copy-start.3 = (bf16[128,448]{0,1:T(8,128)(2,1)S(1)}, bf16[128,448]{0,1:T(8,128)(2,1)}, u32[]{:S(2)}) copy-start(bf16[128,448]{0,1:T(8,128)(2,1)} %param.11) | copy-start | bytes 344068
Sparse Core Ops, SparseCore 0:
  10.9 79.2 all-reduce.2
  94.2 179.6 all-gather.3
  277.7 269.3 all-gather.5
  630.2 65.3 all-reduce.4
where the time goes:
time: 784 us; the launch traced here: 782 us
  waiting for transfers between devices  528 us (67%)
  blocking collectives  140 us (18%)
  other arithmetic  73.2 us (9%)
  local copies, waits for them, and re-layouts  18 us (2%)
  between operations  13.9 us (2%)
    all_gather x2, waiting for transfers between devices, prefix(): gathered = lax.all_gather(part, axis)  450 us
    psum x1, blocking collectives, body(): decoder_bias_grad = lax.psum(jnp.sum(scaled_error, axis=0), 'lat')  140 us
    psum x1, waiting for transfers between devices, body(): preacts = lax.psum(encoder_part, 'wid') + encoder_bias  78.9 us
    add x63, other arithmetic, add_terms(): return earlier + later  63.4 us
    while x3, local copies, waits for them, and re-layouts, prefix(): return lax.fori_loop(0, ahead, one, state)  16.8 us
  transfers between devices with their start and end apart: 4, of which 3 were waited for; matrix products, arithmetic and copies ran while one was open for 1% of the time, Pallas kernels for 0%

commit v1 on v0

--- a/solution.py
+++ b/solution.py
@@ -30,7 +30,12 @@
     latent_ids = first_latent + jnp.arange(latent_width, dtype=jnp.int32)
     kept_float = kept_mask.astype(jnp.float32)
     encoder_part = jnp.dot(activations, encoder, preferred_element_type=jnp.float32)
-    preacts = lax.psum(encoder_part, "wid") + encoder_bias
+
+    def order_roads(sample, peer_axis):
+        y_new = jax.lax.all_gather(sample, peer_axis)
+        return jnp.sum(y_new, axis=0)
+
+    preacts = order_roads(encoder_part, "wid") + encoder_bias
     codes = (kept_float * preacts).astype(jnp.bfloat16)
     inside_rows = (boundaries > first_latent) & (boundaries <= first_latent + latent_width)
     holds_cut = jnp.any(inside_rows)

time: 784 us -> 742 us (0.946)
  waiting for transfers between devices: 528 us -> 485 us
    psum x1 -> x0, waiting for transfers between devices: 78.9 us -> none  [body(): preacts = lax.psum(encoder_part, 'wid') + encoder_bias]
    all_gather x0 -> x1, waiting for transfers between devices: none -> 36.4 us  [order_roads(): y_new = jax.lax.all_gather(sample, peer_axis)]
where the time goes in v1:
time: 742 us; the launch traced here: 740 us
  waiting for transfers between devices  485 us (65%)
  blocking collectives  140 us (19%)
  other arithmetic  74.1 us (10%)
  local copies, waits for them, and re-layouts  18 us (2%)
  between operations  13.9 us (2%)
    all_gather x2, waiting for transfers between devices, prefix(): gathered = lax.all_gather(part, axis)  449 us
    psum x1, blocking collectives, body(): decoder_bias_grad = lax.psum(jnp.sum(scaled_error, axis=0), 'lat')  140 us
    add x63, other arithmetic, add_terms(): return earlier + later  63.4 us
    all_gather x1, waiting for transfers between devices, order_roads(): y_new = jax.lax.all_gather(sample, peer_axis)  36.4 us
    while x3, local copies, waits for them, and re-layouts, prefix(): return lax.fori_loop(0, ahead, one, state)  16.8 us
  transfers between devices with their start and end apart: 4, of which 3 were waited for; matrix products, arithmetic and copies ran while one was open for 1% of the time, Pallas kernels for 0%

profile of v1, /device:TPU:32, one launch (start us, length us, event | category | flops | bytes accessed | tf_op | source)
XLA Modules:
  0.0 739.6 jit_solution(13081505204496175749)
XLA Ops:
  7.2 2.1 fusion.19
  9.4 1.3 select_reduce_fusion
  11.4 36.4 %all-gather.8.cloned.1.call-done = f32[1024,512]{1,0:T(8,128)} async-done(((f32[128,512]{1,0:T(8,128)}), f32[1024,512]{1,0:T(8,128)}) %all-gather.8.cloned.1.call-update) | async-done | bytes 2097168 | tf_op jit(solution)/shard_map/all_gather | solution.py:35
  47.7 1.8 reduce_sum.37
  49.5 1.0 select_bitcast_fusion.1
  51.7 1.3 fusion.16
  53.0 179.6 %all-gather.6.cloned.1.call-done = f32[64,128,448]{1,2,0:T(8,128)} async-done(((f32[1,128,448]{1,2,0:T(8,128)}), f32[64,128,448]{1,2,0:T(8,128)}) %all-gather.6.cloned.1.call-update) | async-done | bytes 14680080 | tf_op jit(solution)/shard_map/all_gather | solution.py:13
  232.6 1.2 while.22
  234.0 1.5 fusion.17
  235.6 269.5 %all-gather.10.cloned.1.call-done = f32[8192,448]{0,1:T(8,128)} async-done(((f32[128,448]{0,1:T(8,128)}), f32[8192,448]{0,1:T(8,128)}) %all-gather.10.cloned.1.call-update) | async-done | bytes 14680080 | tf_op jit(solution)/shard_map/all_gather | solution.py:13
  505.0 16.6 %copy.25 = f32[8192,448]{1,0:T(8,128)} copy(f32[8192,448]{0,1:T(8,128)} %all-gather.10.cloned.1.call-done) | data formatting | bytes 29360128 | tf_op jit(solution)/shard_map/while | solution.py:20
  521.6 65.1 %while.23 = (s32[]{:T(128)}, f32[128,448]{1,0:T(8,128)S(1)}, s32[]{:T(128)}, f32[64,128,448]{2,1,0:T(8,128)}, s32[]{:T(128)}, /*index=5*/s32[]{:T(128)}, s32[]{:T(128)}, s32[]{:T(128)}) while((s32[]{:T(128)}, f32[128,448]{1,0:T(8,128)S(1)}, s32[]{:T(128)}, f32[64,128,448]{2,1,0:T(8,128)}, s32[]{:T(128)}, /*index=5*/s32[]{:T(128)}, s32[]{:T(128)}, ...), condition=%wide.region_6.7_spmd, body=%wide.region_5.6_spmd.sunk | while | flops 57350 | bytes 688263 | solution.py:20
  521.6 1.0 bitcast_add_fusion.6
  522.7 1.0 bitcast_add_fusion.6
  523.7 1.0 bitcast_add_fusion.6
  524.8 1.0 bitcast_add_fusion.6
  525.8 1.0 bitcast_add_fusion.6
  526.9 1.0 bitcast_add_fusion.6
  527.9 1.0 bitcast_add_fusion.6
  529.0 1.0 bitcast_add_fusion.6
  530.0 1.0 bitcast_add_fusion.6
  531.1 1.0 bitcast_add_fusion.6
  532.1 1.0 bitcast_add_fusion.6
  533.2 1.0 bitcast_add_fusion.6
  534.2 1.0 bitcast_add_fusion.6
  535.3 1.0 bitcast_add_fusion.6
  536.3 1.0 bitcast_add_fusion.6
  537.4 1.0 bitcast_add_fusion.6
  538.4 1.0 bitcast_add_fusion.6
  539.5 1.0 bitcast_add_fusion.6
  540.5 1.0 bitcast_add_fusion.6
  541.6 1.0 bitcast_add_fusion.6
  542.6 1.0 bitcast_add_fusion.6
  543.7 1.0 bitcast_add_fusion.6
  544.7 1.0 bitcast_add_fusion.6
  545.8 1.0 bitcast_add_fusion.6
  546.8 1.0 bitcast_add_fusion.6
  547.9 1.0 bitcast_add_fusion.6
  548.9 1.0 bitcast_add_fusion.6
  550.0 1.0 bitcast_add_fusion.6
  551.0 1.0 bitcast_add_fusion.6
  552.1 1.0 bitcast_add_fusion.6
  553.1 1.0 bitcast_add_fusion.6
  554.2 1.0 bitcast_add_fusion.6
  555.2 1.0 bitcast_add_fusion.6
  556.3 1.0 bitcast_add_fusion.6
  557.3 1.0 bitcast_add_fusion.6
  558.4 1.0 bitcast_add_fusion.6
  559.4 1.0 bitcast_add_fusion.6
  560.5 1.0 bitcast_add_fusion.6
  561.5 1.0 bitcast_add_fusion.6
  562.6 1.0 bitcast_add_fusion.6
  563.6 1.0 bitcast_add_fusion.6
  564.7 1.0 bitcast_add_fusion.6
  565.7 1.0 bitcast_add_fusion.6
  567.8 1.0 bitcast_add_fusion.6
  571.0 1.0 bitcast_add_fusion.6
  574.1 1.0 bitcast_add_fusion.6
  581.5 1.0 bitcast_add_fusion.6
  584.6 1.0 bitcast_add_fusion.6
  588.0 140.5 %psum.15 = f32[448]{0:T(512)} all-reduce(f32[448]{0:T(512)S(1)} %get-tuple-element.117), channel_id=1, replica_groups=mesh['lat'=64,'wid'=8] {'lat'}, use_global_device_ids=true, to_apply=%region_10.11 | all-reduce | flops 448 | bytes 3584 | tf_op jit(solution)/shard_map/psum | solution.py:76
  728.4 1.1 fusion
  729.5 2.0 fusion.1
  731.5 1.6 fusion.11
  (47 shorter events, 18.8 us)
Async XLA Ops:
  7.2 43.4 %copy-start = (bf16[512,448]{0,1:T(8,128)(2,1)S(1)}, bf16[512,448]{0,1:T(8,128)(2,1)}, u32[]{:S(2)}) copy-start(bf16[512,448]{0,1:T(8,128)(2,1)} %param.14) | copy-start | bytes 1376260
  7.2 226.8 %copy-start.3 = (bf16[128,448]{0,1:T(8,128)(2,1)S(1)}, bf16[128,448]{0,1:T(8,128)(2,1)}, u32[]{:S(2)}) copy-start(bf16[128,448]{0,1:T(8,128)(2,1)} %param.11) | copy-start | bytes 344068
  7.2 226.8 %copy-start.4 = (f32[448]{0:T(512)S(1)}, f32[448]{0:T(512)}, u32[]{:S(2)}) copy-start(f32[448]{0:T(512)} %param.15) | copy-start | bytes 5380
  7.2 40.5 %all-gather.8.cloned.1.call-start = ((), (), s32[]{:S(2)}) async-start(), calls=%async_computation.2 | async-start | bytes 2359296 | tf_op jit(solution)/shard_map/all_gather | solution.py:35
  9.3 223.3 %all-gather.6.cloned.1.call-start = ((), (), s32[]{:S(2)}) async-start(), calls=%async_computation | async-start | bytes 14909440 | tf_op jit(solution)/shard_map/all_gather | solution.py:13
  51.7 453.4 %all-gather.10.cloned.1.call-start = ((), (), s32[]{:S(2)}) async-start(), calls=%async_computation.3 | async-start | bytes 14909440 | tf_op jit(solution)/shard_map/all_gather | solution.py:13
  235.5 494.0 %all-reduce.2.cloned.1.call-start = ((), (), s32[]{:S(2)}) async-start(), calls=%async_computation.1 | async-start | bytes 524288 | tf_op jit(solution)/shard_map/psum | solution.py:66
  235.5 351.3 %copy-start.2 = (f32[128,448]{0,1:T(8,128)S(1)}, f32[128,448]{0,1:T(8,128)}, u32[]{:S(2)}) copy-start(f32[128,448]{0,1:T(8,128)} %get-tuple-element.118) | copy-start | bytes 688132
  235.6 493.9 %copy-start.1 = (s32[128,512]{1,0:T(8,128)S(1)}, s32[128,512]{1,0:T(8,128)}, u32[]{:S(2)}) copy-start(s32[128,512]{1,0:T(8,128)} %param.16) | copy-start | bytes 786436
Sparse Core Ops, SparseCore 0:
  10.8 36.9 all-gather.7
  51.8 180.7 all-gather.5
  236.1 268.8 all-gather.9
  588.1 65.3 all-reduce.1
